TPU v7x, 256 devices: a whole 4x4x8 slice. The times are simulated.
256 devices in a mesh: beads: 64 (over x, y, z_hi, core), waves: 4 (over z_lo).
Axes of the slice: x: 4, y: 4, z: 8 (z_hi: 2, z_lo: 4; z = z_hi * 4 + z_lo), core: 2. Of those that a mesh axis runs over, the one named last changes fastest.
Arguments:
- positions: float32 [3, 32768], P(None, 'beads'), may hold values from 0 to 256
- features: bfloat16 [32768, 256], P(('beads', 'waves')), may hold values from -6 to 6
- cotangent: bfloat16 [32768, 256], P(('beads', 'waves')), may hold values from -6 to 6
- wavevectors: float32 [3, 4096], replicated, may hold values from -0.25 to 0.25
- filter_gain: bfloat16 [4096, 256], P(('beads', 'waves')), may hold values from -6 to 6
Outputs:
- grad_features: bfloat16 [32768, 256], P(('beads', 'waves'))
- grad_positions: float32 [3, 32768], P(None, ('beads', 'waves'))
- grad_filter: float32 [4096, 256], P(('beads', 'waves'))
All inputs are finite; a program needn't handle non-finite values.
Results may differ from a plain program's by a relative error of at most 0.012.
Values may be sent and summed in bfloat16 or wider, within the bound.
No kernel may reach another device: no remote copies, remote signals or barrier semaphores. Data moves between devices by JAX's collectives and lax.ppermute only.
A program may use at most 64 MiB of HBM per device.

v0:
```python
import math

import jax
import jax.numpy as jnp
from jax import lax
from jax.experimental import pallas as pl
from jax.experimental.pallas import tpu as pltpu
from jax.sharding import Mesh
from jax.sharding import PartitionSpec as P


ALL = ("x", "y", "zh", "core", "zl")
Z = ("zh", "zl")
XY = ("x", "y")
BF16 = jnp.bfloat16
F32 = jnp.float32
LANES = 128

SIN_TURN = (6.28318501, -41.3416557, 81.6010056, -76.5497818, 39.536705)


def sin_turn(h):
    s = h * h
    poly = SIN_TURN[-1]
    for c in SIN_TURN[-2::-1]:
        poly = poly * s + c
    return poly * h


def load_kernel(cot, feat, pos, wv, own, sent, pos_near, wv_near, sems):
    beads, width = cot.shape
    copies = [
        pltpu.make_async_copy(cot, own.at[:, :width], sems.at[0]),
        pltpu.make_async_copy(feat, own.at[:, width:], sems.at[1]),
        pltpu.make_async_copy(pos, pos_near, sems.at[2]),
        pltpu.make_async_copy(wv, wv_near, sems.at[3]),
    ]
    for c in copies:
        c.start()
    for c in copies:
        c.wait()
    sent[:beads, :] = own[...]
    left = pos_near[...]
    parts = []
    for _ in range(3):
        part = left.astype(BF16).astype(F32)
        parts.append(part)
        left = left - part
    parts.append(jnp.zeros((7, left.shape[1]), F32))
    sent[beads:, :] = jnp.concatenate(parts, 0).astype(BF16)


def trig_rows(kcols, pos, cs, zh, zl, first):
    n_xy = cs.shape[1]
    n_z = cs.shape[4] // LANES
    n_zl = n_z // 2
    columns = [
        pl.multiple_of(lax.rem(zh * n_zl + zl + n_z - first - i, n_z) * LANES, LANES)
        for i in range(n_zl)
    ]

    def step(i, carry):
        dc, xy = i // n_xy, lax.rem(i, n_xy)
        cols = kcols[pl.ds(pl.multiple_of(i * 16, 16), 16), :]
        t = cols[:, 0:1] * pos[0:1] + cols[:, 1:2] * pos[1:2] + cols[:, 2:3] * pos[2:3]
        f = t - jnp.round(t)
        cosine = sin_turn(0.25 - jnp.abs(f)).astype(BF16)
        sine = sin_turn(jnp.maximum(jnp.minimum(f, 0.5 - f), -0.5 - f)).astype(BF16)
        for j, column in enumerate(columns):
            part = slice(j * LANES, (j + 1) * LANES)
            cs[dc, xy, 0, :, pl.ds(column, LANES)] = cosine[:, part]
            cs[dc, xy, 1, :, pl.ds(column, LANES)] = sine[:, part]
        return carry

    lax.fori_loop(0, 2 * n_xy, step, 0, unroll=4)


def trig_near_kernel(scal, pos, wv, cs, kvrel, kcols, kvt):
    zh, zl, core = scal[0], scal[1], scal[2]
    n_xy = cs.shape[1]
    n_zl = cs.shape[4] // LANES // 2
    for xy in range(n_xy):
        at = pl.multiple_of((xy * 2 + zh) * LANES, LANES)
        piece = wv[:, pl.ds(at, LANES)]
        piece = jnp.concatenate([piece, jnp.zeros((5, LANES), F32)], 0)
        kvt[xy, :, 0:8] = piece.T
    for dc in range(2):
        at = pl.multiple_of((jnp.bitwise_xor(core, dc) * n_zl + zl) * 16, 16)
        for xy in range(n_xy):
            cols = kvt[xy, pl.ds(at, 16), 0:8]
            rows = slice((dc * n_xy + xy) * 16, (dc * n_xy + xy + 1) * 16)
            hi = cols.astype(BF16)
            lo = (cols - hi.astype(F32)).astype(BF16)
            kvrel[rows, :] = jnp.concatenate([hi, lo], 1)
            kcols[rows, :] = cols * (1.0 / (2.0 * math.pi))
    trig_rows(kcols, pos[...], cs, zh, zl, zh * n_zl)


def trig_far_kernel(scal, ahead, behind, kcols, _, cs):
    zh, zl = scal[0], scal[1]
    n_zl = cs.shape[4] // LANES // 2
    beads = ahead.shape[0] - 16
    rows = jnp.where(zl < n_zl // 2, ahead[beads:, :], behind[beads:, :]).astype(F32)
    pos = rows[0:3] + rows[3:6] + rows[6:9]
    trig_rows(kcols, pos, cs, zh, zl, jnp.bitwise_xor(zh, 1) * n_zl)


def joined(pieces):
    return jnp.concatenate([p[:LANES] for p in pieces], 0)


def early_kernel(cs, *refs):
    pieces, out = refs[:-1], refs[-1]
    rows = cs[...].reshape(-1, cs.shape[4])
    n = 3 * LANES
    near = jnp.dot(rows[:, :n], joined(pieces[:3]), preferred_element_type=F32)
    m = rows.shape[1] - 2 * LANES
    near += jnp.dot(rows[:, m:], joined(pieces[3:]), preferred_element_type=F32)
    out[...] = near.reshape(out.shape)


def late_kernel(dc, cs, early, *refs):
    pieces, out = refs[:-1], refs[-1]
    rows = cs[dc].reshape(-1, cs.shape[4])
    m = rows.shape[1] - 2 * LANES
    part = jnp.dot(rows[:, 3 * LANES : m], joined(pieces), preferred_element_type=F32)
    out[...] = (part.reshape(out.shape) + early[dc]).astype(out.dtype)


def filter_kernel(spec_scale, wave_scale, arrived, gain, out, grad_filter):
    n = arrived.shape[0]
    width = gain.shape[1]
    total = arrived[0].astype(F32)
    for i in range(1, n):
        total = total + arrived[i].astype(F32)
    total = total.reshape(2, 16, 2 * width)
    cot = total[:, :, :width] * wave_scale
    spec = total[:, :, width:] * spec_scale
    g = gain[...].astype(F32)
    grad_filter[...] = cot[0] * spec[0] + cot[1] * spec[1]
    filt = (g[None] * spec * (wave_scale / spec_scale)).astype(BF16)
    dspec = (g[None] * cot).astype(BF16)
    both = jnp.concatenate([filt, dspec], 2).reshape(32, 2 * width)
    for i in range(n):
        out[i] = both


def half_gradients(dc, cs, kvrel, stacked, beads_all):
    n_xy, beads = cs.shape[1], cs.shape[4]
    width = beads_all.shape[1] // 2
    both = stacked[...].reshape(n_xy * 32, 2 * width)
    ab = lax.dot_general(both, beads_all, (((1,), (1,)), ((), ())), preferred_element_type=F32)
    ab = ab.reshape(n_xy, 2, 16, beads)
    d = cs[dc, :, 0].astype(F32) * ab[:, 1] - cs[dc, :, 1].astype(F32) * ab[:, 0]
    d = d.reshape(n_xy * 16, beads).astype(BF16)
    kv = kvrel[dc * n_xy * 16 : (dc + 1) * n_xy * 16, :]
    gp = lax.dot_general(kv, d, (((0,), (0,)), ((), ())), preferred_element_type=F32)
    rows = cs[dc].reshape(n_xy * 32, beads)
    gf = lax.dot_general(
        both[:, width:], rows, (((0,), (0,)), ((), ())), preferred_element_type=F32
    )
    return gf, gp[0:8] + gp[8:16]


def grads_near_kernel(cs, kvrel, stacked, *refs):
    pieces, (gf_out, gp_out) = refs[:-2], refs[-2:]
    beads_all = joined(pieces)
    gf, gp = half_gradients(0, cs, kvrel, stacked, beads_all)
    gf_out[...] = gf
    gp_out[...] = gp


def grads_far_kernel(spec_scale, scal, cs, kvrel, stacked, gf_in, gp_in, *refs):
    pieces, out = refs[:-1], refs[-1]
    beads_all = joined(pieces)
    gf, gp = half_gradients(1, cs, kvrel, stacked, beads_all)
    gf = ((gf + gf_in[...]) * spec_scale).astype(BF16)
    gp = (gp + gp_in[...]) * spec_scale
    hi = gp.astype(BF16).astype(F32)
    tail = jnp.concatenate([hi[0:3], (gp - hi)[0:3], jnp.zeros_like(gp[0:2])], 0).astype(BF16)
    n_z = out.shape[0]
    width = gf.shape[0]
    here = scal[0] * (n_z // 2) + scal[1]
    for shift in range(n_z):
        at = slice(shift * LANES, (shift + 1) * LANES)
        to = lax.rem(here + n_z - shift, n_z)
        out[to, 0:width, :] = gf[:, at]
        out[to, width : width + 8, :] = tail[:, at]


def total_kernel(arrived, gf_out, gp_out):
    total = arrived[0].astype(F32)
    for i in range(1, arrived.shape[0]):
        total = total + arrived[i].astype(F32)
    width = gf_out.shape[1]
    gf_out[...] = total[:width].T.astype(BF16)
    gp_out[...] = total[width : width + 3] + total[width + 3 : width + 6]


def call(kernel, out_shape, n_in, scalars=0, scratch=(), aliases=None, space=pltpu.VMEM):
    specs = [pl.BlockSpec(memory_space=pltpu.SMEM)] * scalars
    specs += [pl.BlockSpec(memory_space=space)] * (n_in - scalars)
    outs = jax.tree.map(lambda _: pl.BlockSpec(memory_space=pltpu.VMEM), out_shape)
    return pl.pallas_call(
        kernel,
        out_shape=out_shape,
        in_specs=specs,
        out_specs=outs,
        scratch_shapes=scratch,
        input_output_aliases=aliases or {},
        compiler_params=pltpu.CompilerParams(vmem_limit_bytes=16 << 20),
    )


def shape(dims, dtype):
    return jax.ShapeDtypeStruct(dims, dtype)


def body(positions, features, cotangent, wavevectors, filter_gain):
    n_z = lax.axis_size(Z)
    n_xy = lax.axis_size(XY)
    beads_dev, width = features.shape
    beads_grp = beads_dev * n_z
    n_beads = beads_grp * n_xy * 2
    spec_scale = 1.0 / math.sqrt(n_beads)
    wave_scale = 1.0 / math.sqrt(wavevectors.shape[1])

    def along_z(a, k):
        return lax.ppermute(a, Z, [(i, (i + k) % n_z) for i in range(n_z)])

    def across(a):
        return lax.ppermute(a, "core", [(0, 1), (1, 0)])

    inputs = (cotangent, features, positions, wavevectors)
    inputs = [pltpu.with_memory_space_constraint(a, pltpu.HBM) for a in inputs]
    own, sent, pos_near, wv_near = call(
        load_kernel,
        (
            shape((beads_dev, 2 * width), BF16),
            shape((beads_dev + 16, 2 * width), BF16),
            shape(positions.shape, F32),
            shape(wavevectors.shape, F32),
        ),
        4,
        scratch=[pltpu.SemaphoreType.DMA((4,))],
        space=pltpu.HBM,
    )(*inputs)
    pieces = {0: own, 2: along_z(sent, 2), 6: along_z(sent, -2)}

    scal = jnp.stack([lax.axis_index("zh"), lax.axis_index("zl"), lax.axis_index("core")])
    scal = scal.astype(jnp.int32)
    n_rows = 2 * n_xy * 16
    cs_shape = shape((2, n_xy, 2, 16, beads_grp), BF16)
    trig = call(
        trig_near_kernel,
        (cs_shape, shape((n_rows, 16), BF16), shape((n_rows, 8), F32)),
        3,
        scalars=1,
        scratch=[pltpu.VMEM((n_xy, LANES, 8), F32)],
    )(scal, pos_near, wv_near)
    own, trig = lax.optimization_barrier((own, trig))
    pieces[1], pieces[7] = along_z(own, 1), along_z(own, -1)
    pieces[2], pieces[6], trig = lax.optimization_barrier((pieces[2], pieces[6], trig))
    ahead, behind = pieces[2][:beads_dev], pieces[6][:beads_dev]
    onward = jnp.where(lax.axis_index("core") == 0, ahead, behind)
    n_zl = lax.axis_size("zl")

    def at(z, core):
        return (z // n_zl * 2 + core) * n_zl + z % n_zl

    pairs = [(at(z, c), at((z + 2 - 4 * c) % n_z, c)) for z in range(n_z) for c in range(2)]
    pieces[4] = lax.ppermute(onward, ("zh", "core", "zl"), pairs)
    pieces[3], pieces[5] = along_z(ahead, 1), along_z(behind, -1)
    late_blocks = [pieces[3], pieces[4], pieces[5]]
    blocks = [pieces[k] for k in range(n_z)]
    cs = call(trig_far_kernel, cs_shape, 5, scalars=1, aliases={4: 0})(
        scal, pieces[2], pieces[6], trig[2], trig[0]
    )
    kvrel = trig[1]

    near_blocks = blocks[:3] + blocks[-2:]
    early = call(
        early_kernel, shape((2, n_xy, 32, 2 * width), F32), 1 + len(near_blocks)
    )(cs, *near_blocks)

    def spectra(dc, dtype):
        return call(
            lambda *refs: late_kernel(dc, *refs),
            shape((n_xy, 32, 2 * width), dtype),
            2 + len(late_blocks),
        )(cs, early, *late_blocks)

    theirs = across(spectra(1, BF16))
    mine = (spectra(0, F32) + theirs.astype(F32)).astype(BF16)
    arrived = lax.all_to_all(mine, XY, 0, 0, tiled=True)
    copies, grad_filter = call(
        lambda *refs: filter_kernel(spec_scale, wave_scale, *refs),
        (shape((n_xy, 32, 2 * width), BF16), shape((16, width), F32)),
        2,
    )(arrived, filter_gain)
    near = lax.all_to_all(copies, XY, 0, 0, tiled=True)
    far = across(near)
    gf, gp = call(
        grads_near_kernel,
        (shape((width, beads_grp), F32), shape((8, beads_grp), F32)),
        3 + len(blocks),
    )(cs, kvrel, near, *blocks)
    parts = call(
        lambda *refs: grads_far_kernel(spec_scale, *refs),
        shape((n_z, width + 8, beads_dev), BF16),
        6 + len(blocks),
        scalars=1,
    )(scal, cs, kvrel, far, gf, gp, *blocks)
    grad_feat, grad_pos = call(
        total_kernel, (shape((beads_dev, width), BF16), shape((3, beads_dev), F32)), 1
    )(lax.all_to_all(parts, Z, 0, 0, tiled=True))
    return grad_feat, grad_pos, grad_filter


def solution(mesh):
    torus = Mesh(mesh.devices.reshape(4, 4, 2, 2, mesh.shape["waves"]), ALL)
    beads = ("x", "y", "zh", "core")
    return jax.shard_map(
        body,
        mesh=torus,
        in_specs=(P(None, beads), P(ALL, None), P(ALL, None), P(), P(ALL, None)),
        out_specs=(P(ALL, None), P(None, ALL), P(ALL, None)),
        check_vma=False,
    )
```

profile of v0, /device:TPU:8, one launch (start us, length us, event | category | flops | bytes accessed | tf_op | source)
XLA Modules:
  0.0 90.3 jit_solution(10125387231917204979)
XLA Ops:
  0.6 1.0 %shard_map.76 = (bf16[128,512]{1,0:T(8,128)(2,1)S(1)}, bf16[144,512]{1,0:T(8,128)(2,1)S(1)}, f32[3,512]{1,0:T(4,128)S(1)}, f32[3,4096]{1,0:T(4,128)S(1)}) custom-call(bf16[128,256]{1,0:T(8,128)(2,1)} %cot.1, bf16[128,256]{1,0:T(8,128)(2,1)} %feat.1, f32[3,512]{1,0:T(4,128)} %pos.1, f32[3,4096]{1,0:T(4,128)} %wv.1), custom_call_target="tpu_custom_call" | custom-call | tf_op jit(solution)/shard_map/pallas_call | solution.py:236
  1.6 6.4 %collective-permute-start.1 = (bf16[144,512]{1,0:T(8,128)(2,1)S(1)}, bf16[144,512]{1,0:T(8,128)(2,1)S(1)}, u32[]{:S(2)}, u32[]{:S(2)}) collective-permute-start(bf16[144,512]{1,0:T(8,128)(2,1)S(1)} %get-tuple-element.25), channel_id=1, source_target_pairs={{0,10},{1,11},{2,0},{3,1},{8,2},{9,3},{10,8},{11,9},{4,14},{5,15},... | collective-permute-start | bytes 442376 | tf_op jit(solution)/shard_map/ppermute | solution.py:229
  8.0 0.0 collective-permute-start
  8.0 0.1 pad_add_fusion.scal.refs_0_
  8.1 2.8 %shard_map.77 = (bf16[2,16,2,16,1024]{4,3,2,1,0:T(8,128)(2,1)S(1)}, bf16[512,16]{1,0:T(8,128)(2,1)S(1)}, f32[512,8]{1,0:T(8,128)S(1)}) custom-call(s32[3]{0:T(128)S(1)} %pad_add_fusion.scal.refs_0_, f32[3,512]{1,0:T(4,128)S(1)} %get-tuple-element.27.pos, f32[3,4096]{1,0:T(4,128)S(1)} %get-tuple-element.28.wv), custom_call_target="tpu_custom_call" | custom-call | tf_op jit(solution)/shard_map/pallas_call | solution.py:254
  10.9 3.8 %collective-permute-start.3 = (bf16[128,512]{1,0:T(8,128)(2,1)S(1)}, bf16[128,512]{1,0:T(8,128)(2,1)S(1)}, u32[]{:S(2)}, u32[]{:S(2)}) collective-permute-start(bf16[128,512]{1,0:T(8,128)(2,1)S(1)} %get-tuple-element.40.refs_0_.refs_6_), channel_id=1, source_target_pairs={{0,11},{1,0},{2,1},{3,2},{8,3},{9,8},{10,9},{11,10},{4,15},{5,4},{... | collective-permute-start | bytes 393224 | tf_op jit(solution)/shard_map/ppermute | solution.py:229
  14.7 0.0 collective-permute-start.2
  14.7 0.0 collective-permute-done.1.behind.refs_3_.refs_6_.refs_12_
  14.7 3.2 %collective-permute-done.ahead.refs_2_.refs_8_ = bf16[144,512]{1,0:T(8,128)(2,1)S(1)} collective-permute-done((bf16[144,512]{1,0:T(8,128)(2,1)S(1)}, bf16[144,512]{1,0:T(8,128)(2,1)S(1)}, u32[]{:S(2)}, u32[]{:S(2)}) %collective-permute-start) | collective-permute-done | bytes 147488 | tf_op jit(solution)/shard_map/ppermute | solution.py:229
  17.9 1.2 %collective-permute-start.6 = (bf16[128,512]{1,0:T(8,128)(2,1)S(1)}, bf16[128,512]{1,0:T(8,128)(2,1)S(1)}, u32[]{:S(2)}, u32[]{:S(2)}) collective-permute-start(bf16[128,512]{1,0:T(8,128)(2,1)S(1)} %get-tuple-element.47), channel_id=1, source_target_pairs={{0,11},{1,0},{2,1},{3,2},{8,3},{9,8},{10,9},{11,10},{4,15},{5,4},{... | collective-permute-start | bytes 393224 | tf_op jit(solution)/shard_map/ppermute | solution.py:229
  19.1 2.7 %collective-permute-start.5 = (bf16[128,512]{1,0:T(8,128)(2,1)S(1)}, bf16[128,512]{1,0:T(8,128)(2,1)S(1)}, u32[]{:S(2)}, u32[]{:S(2)}) collective-permute-start(bf16[128,512]{1,0:T(8,128)(2,1)S(1)} %get-tuple-element.48), channel_id=1, source_target_pairs={{0,2},{4,14},{1,3},{5,15},{2,8},{6,4},{3,9},{7,5},{8,10},{12,6},{9... | collective-permute-start | bytes 393224 | tf_op jit(solution)/shard_map/ppermute | solution.py:272
  21.7 0.0 collective-permute-start.4
  21.7 2.4 %shard_map.78.cs.refs_0_.refs_1_ = bf16[2,16,2,16,1024]{4,3,2,1,0:T(8,128)(2,1)S(1)} custom-call(s32[3]{0:T(128)S(1)} %pad_add_fusion.scal.refs_0_, bf16[144,512]{1,0:T(8,128)(2,1)S(1)} %collective-permute-done.ahead.refs_2_.refs_8_, bf16[144,512]{1,0:T(8,128)(2,1)S(1)} %collective-permute-done.1.behind.refs_3_.refs_6_.refs_12_, ...), custom_call_target="tpu_custom_call", output_to_operand_aliasing={{}: (4, {})} | custom-call | tf_op jit(solution)/shard_map/pallas_call | solution.py:276
  24.1 0.0 collective-permute-done.3.refs_4_.refs_7_.refs_13_
  24.1 0.0 collective-permute-done.2.refs_1_.refs_7_
  24.1 1.0 %shard_map.79.refs_1_ = f32[2,16,32,512]{3,2,1,0:T(8,128)S(1)} custom-call(bf16[2,16,2,16,1024]{4,3,2,1,0:T(8,128)(2,1)S(1)} %shard_map.78.cs.refs_0_.refs_1_, bf16[128,512]{1,0:T(8,128)(2,1)S(1)} %get-tuple-element.40.refs_0_.refs_6_, bf16[128,512]{1,0:T(8,128)(2,1)S(1)} %collective-permute-done.2.refs_1_.refs_7_, ...), custom_call_target="tpu_custom_call" | custom-call | tf_op jit(solution)/shard_map/pallas_call | solution.py:282
  25.1 0.0 collective-permute-done.6.refs_4_.refs_5_.refs_11_
  25.1 1.7 %collective-permute-done.5.refs_3_.refs_4_.refs_10_ = bf16[128,512]{1,0:T(8,128)(2,1)S(1)} collective-permute-done((bf16[128,512]{1,0:T(8,128)(2,1)S(1)}, bf16[128,512]{1,0:T(8,128)(2,1)S(1)}, u32[]{:S(2)}, u32[]{:S(2)}) %collective-permute-start.5) | collective-permute-done | bytes 131104 | tf_op jit(solution)/shard_map/ppermute | solution.py:272
  26.8 1.9 %collective-permute-done.4.refs_2_.refs_3_.refs_9_ = bf16[128,512]{1,0:T(8,128)(2,1)S(1)} collective-permute-done((bf16[128,512]{1,0:T(8,128)(2,1)S(1)}, bf16[128,512]{1,0:T(8,128)(2,1)S(1)}, u32[]{:S(2)}, u32[]{:S(2)}) %collective-permute-start.4) | collective-permute-done | bytes 131104 | tf_op jit(solution)/shard_map/ppermute | solution.py:229
  28.8 0.4 shard_map.81
  29.2 0.1 collective-permute-start.7
  29.3 0.4 shard_map.80
  29.8 0.0 copy-start
  29.8 1.4 %collective-permute-done.7 = bf16[16,32,512]{2,1,0:T(8,128)(2,1)S(1)} collective-permute-done((bf16[16,32,512]{2,1,0:T(8,128)(2,1)S(1)}, bf16[16,32,512]{2,1,0:T(8,128)(2,1)S(1)}, u32[]{:S(2)}, u32[]{:S(2)}) %collective-permute-start.7) | collective-permute-done | bytes 524320 | tf_op jit(solution)/shard_map/ppermute | solution.py:232
  31.2 0.2 add_convert_fusion
  31.4 17.6 %all_to_all.15.refs_0_ = bf16[16,32,512]{2,1,0:T(8,128)(2,1)S(1)} all-to-all(bf16[16,32,512]{2,1,0:T(8,128)(2,1)S(1)} %add_convert_fusion), channel_id=1, replica_groups=mesh['x'=4,'y'=4,'zh'=2,'core'=2,'zl'=4] {'x','y'}, dimensions={0} | all-to-all | bytes 1048576 | tf_op jit(solution)/shard_map/all_to_all | solution.py:295
  49.0 0.0 copy-done
  49.0 0.7 shard_map.82
  49.8 13.9 %all_to_all.16.stacked = bf16[16,32,512]{2,1,0:T(8,128)(2,1)S(1)} all-to-all(bf16[16,32,512]{2,1,0:T(8,128)(2,1)S(1)} %get-tuple-element.41), channel_id=1, replica_groups=mesh['x'=4,'y'=4,'zh'=2,'core'=2,'zl'=4] {'x','y'}, dimensions={0} | all-to-all | bytes 1048576 | tf_op jit(solution)/shard_map/all_to_all | solution.py:301
  63.7 0.0 collective-permute-start.8
  63.7 1.2 %shard_map.83 = (f32[256,1024]{1,0:T(8,128)S(1)}, f32[8,1024]{1,0:T(8,128)S(1)}) custom-call(bf16[2,16,2,16,1024]{4,3,2,1,0:T(8,128)(2,1)S(1)} %shard_map.78.cs.refs_0_.refs_1_, bf16[512,16]{1,0:T(8,128)(2,1)S(1)} %get-tuple-element.39.kvrel.refs_2_, bf16[16,32,512]{2,1,0:T(8,128)(2,1)S(1)} %all_to_all.16.stacked, ...), custom_call_target="tpu_custom_call" | custom-call | tf_op jit(solution)/shard_map/pallas_call | solution.py:303
  64.9 0.7 collective-permute-done.8.refs_3_
  65.6 1.8 %shard_map.84 = bf16[8,264,128]{2,1,0:T(8,128)(2,1)S(1)} custom-call(s32[3]{0:T(128)S(1)} %pad_add_fusion.scal.refs_0_, bf16[2,16,2,16,1024]{4,3,2,1,0:T(8,128)(2,1)S(1)} %shard_map.78.cs.refs_0_.refs_1_, bf16[512,16]{1,0:T(8,128)(2,1)S(1)} %get-tuple-element.39.kvrel.refs_2_, bf16[16,32,512]{2,1,0:T(8,128)(2,1)S(1)} %collective-permute-done.8.refs_3_, ...), custom_call_target="tpu_custom_call" | custom-call | tf_op jit(solution)/shard_map/pallas_call | solution.py:308
  67.3 22.2 %all_to_all.17.arrived = bf16[8,264,128]{2,1,0:T(8,128)(2,1)S(1)} all-to-all(bf16[8,264,128]{2,1,0:T(8,128)(2,1)S(1)} %shard_map.84), channel_id=1, replica_groups=mesh['x'=4,'y'=4,'zh'=2,'core'=2,'zl'=4] {'zh','zl'}, dimensions={0} | all-to-all | bytes 1081344 | tf_op jit(solution)/shard_map/all_to_all | solution.py:316
  89.5 0.8 shard_map.85
  (1 shorter events, 0.0 us)
Async XLA Ops:
  1.6 13.0 %collective-permute-start.1 = (bf16[144,512]{1,0:T(8,128)(2,1)S(1)}, bf16[144,512]{1,0:T(8,128)(2,1)S(1)}, u32[]{:S(2)}, u32[]{:S(2)}) collective-permute-start(bf16[144,512]{1,0:T(8,128)(2,1)S(1)} %get-tuple-element.25), channel_id=1, source_target_pairs={{0,10},{1,11},{2,0},{3,1},{8,2},{9,3},{10,8},{11,9},{4,14},{5,15},... | collective-permute-start | bytes 442376 | tf_op jit(solution)/shard_map/ppermute | solution.py:229
  8.0 9.9 %collective-permute-start = (bf16[144,512]{1,0:T(8,128)(2,1)S(1)}, bf16[144,512]{1,0:T(8,128)(2,1)S(1)}, u32[]{:S(2)}, u32[]{:S(2)}) collective-permute-start(bf16[144,512]{1,0:T(8,128)(2,1)S(1)} %get-tuple-element.25), channel_id=1, source_target_pairs={{0,2},{1,3},{2,8},{3,9},{8,10},{9,11},{10,0},{11,1},{4,6},{5,7},{6... | collective-permute-start | bytes 442376 | tf_op jit(solution)/shard_map/ppermute | solution.py:229
  10.9 13.2 %collective-permute-start.3 = (bf16[128,512]{1,0:T(8,128)(2,1)S(1)}, bf16[128,512]{1,0:T(8,128)(2,1)S(1)}, u32[]{:S(2)}, u32[]{:S(2)}) collective-permute-start(bf16[128,512]{1,0:T(8,128)(2,1)S(1)} %get-tuple-element.40.refs_0_.refs_6_), channel_id=1, source_target_pairs={{0,11},{1,0},{2,1},{3,2},{8,3},{9,8},{10,9},{11,10},{4,15},{5,4},{... | collective-permute-start | bytes 393224 | tf_op jit(solution)/shard_map/ppermute | solution.py:229
  14.7 9.5 %collective-permute-start.2 = (bf16[128,512]{1,0:T(8,128)(2,1)S(1)}, bf16[128,512]{1,0:T(8,128)(2,1)S(1)}, u32[]{:S(2)}, u32[]{:S(2)}) collective-permute-start(bf16[128,512]{1,0:T(8,128)(2,1)S(1)} %get-tuple-element.40.refs_0_.refs_6_), channel_id=1, source_target_pairs={{0,1},{1,2},{2,3},{3,8},{8,9},{9,10},{10,11},{11,0},{4,5},{5,6},{6... | collective-permute-start | bytes 393224 | tf_op jit(solution)/shard_map/ppermute | solution.py:229
  17.9 7.2 %collective-permute-start.6 = (bf16[128,512]{1,0:T(8,128)(2,1)S(1)}, bf16[128,512]{1,0:T(8,128)(2,1)S(1)}, u32[]{:S(2)}, u32[]{:S(2)}) collective-permute-start(bf16[128,512]{1,0:T(8,128)(2,1)S(1)} %get-tuple-element.47), channel_id=1, source_target_pairs={{0,11},{1,0},{2,1},{3,2},{8,3},{9,8},{10,9},{11,10},{4,15},{5,4},{... | collective-permute-start | bytes 393224 | tf_op jit(solution)/shard_map/ppermute | solution.py:229
  19.1 7.8 %collective-permute-start.5 = (bf16[128,512]{1,0:T(8,128)(2,1)S(1)}, bf16[128,512]{1,0:T(8,128)(2,1)S(1)}, u32[]{:S(2)}, u32[]{:S(2)}) collective-permute-start(bf16[128,512]{1,0:T(8,128)(2,1)S(1)} %get-tuple-element.48), channel_id=1, source_target_pairs={{0,2},{4,14},{1,3},{5,15},{2,8},{6,4},{3,9},{7,5},{8,10},{12,6},{9... | collective-permute-start | bytes 393224 | tf_op jit(solution)/shard_map/ppermute | solution.py:272
  21.7 7.1 %collective-permute-start.4 = (bf16[128,512]{1,0:T(8,128)(2,1)S(1)}, bf16[128,512]{1,0:T(8,128)(2,1)S(1)}, u32[]{:S(2)}, u32[]{:S(2)}) collective-permute-start(bf16[128,512]{1,0:T(8,128)(2,1)S(1)} %get-tuple-element.49), channel_id=1, source_target_pairs={{0,1},{1,2},{2,3},{3,8},{8,9},{9,10},{10,11},{11,0},{4,5},{5,6},{6... | collective-permute-start | bytes 393224 | tf_op jit(solution)/shard_map/ppermute | solution.py:229
  29.2 2.0 %collective-permute-start.7 = (bf16[16,32,512]{2,1,0:T(8,128)(2,1)S(1)}, bf16[16,32,512]{2,1,0:T(8,128)(2,1)S(1)}, u32[]{:S(2)}, u32[]{:S(2)}) collective-permute-start(bf16[16,32,512]{2,1,0:T(8,128)(2,1)S(1)} %shard_map.81), channel_id=1, source_target_pairs={{0,4},{4,0},{1,5},{5,1},{2,6},{6,2},{3,7},{7,3},{8,12},{12,8},{9,1... | collective-permute-start | bytes 1572872 | tf_op jit(solution)/shard_map/ppermute | solution.py:232
  29.8 19.3 %copy-start = (bf16[16,256]{1,0:T(8,128)(2,1)S(1)}, bf16[16,256]{1,0:T(8,128)(2,1)}, u32[]{:S(2)}) copy-start(bf16[16,256]{1,0:T(8,128)(2,1)} %refs_1_.1) | copy-start | bytes 24580
  63.7 1.9 %collective-permute-start.8 = (bf16[16,32,512]{2,1,0:T(8,128)(2,1)S(1)}, bf16[16,32,512]{2,1,0:T(8,128)(2,1)S(1)}, u32[]{:S(2)}, u32[]{:S(2)}) collective-permute-start(bf16[16,32,512]{2,1,0:T(8,128)(2,1)S(1)} %all_to_all.16.stacked), channel_id=1, source_target_pairs={{0,4},{4,0},{1,5},{5,1},{2,6},{6,2},{3,7},{7,3},{8,12},{12,8},{9,1... | collective-permute-start | bytes 1572872 | tf_op jit(solution)/shard_map/ppermute | solution.py:232
where the time goes:
time: 91.6 us; the launch traced here: 90.3 us
  blocking collectives  53.7 us (59%)
  starting transfers between devices  14.1 us (15%)
  Pallas kernels  12.4 us (14%)
  waiting for transfers between devices  9.06 us (10%)
    all_to_all x1, blocking collectives, body(): lax.all_to_all(parts, Z, 0, 0, tiled=True)  22.2 us
    all_to_all x1, blocking collectives, body(): arrived = lax.all_to_all(mine, XY, 0, 0, tiled=True)  17.6 us
    all_to_all x1, blocking collectives, body(): near = lax.all_to_all(copies, XY, 0, 0, tiled=True)  13.9 us
    ppermute x6, starting transfers between devices, along_z(): return lax.ppermute(a, Z, [(i, (i + k) % n_z) for i in range(n_z)])  11.3 us
    ppermute x6, waiting for transfers between devices, along_z(): return lax.ppermute(a, Z, [(i, (i + k) % n_z) for i in range(n_z)])  5.17 us
    pallas_call x1, Pallas kernels, body(): call(trig_near_kernel, (cs_shape, shape((n_rows, 16), BF16), shape((n_row...  2.8 us
    ppermute x1, starting transfers between devices, body(): pieces[4] = lax.ppermute(onward, ('zh', 'core', 'zl'), pairs)  2.66 us
    pallas_call x1, Pallas kernels, body(): call(trig_far_kernel, cs_shape, 5, scalars=1, aliases={4: 0})  2.35 us
  transfers between devices with their start and end apart: 9, of which 5 were waited for; matrix products, arithmetic and copies ran while one was open for 0% of the time, Pallas kernels for 9%

commit v1 on v0

--- a/solution.py
+++ b/solution.py
@@ -112,18 +112,17 @@
 def early_kernel(cs, *refs):
     pieces, out = refs[:-1], refs[-1]
     rows = cs[...].reshape(-1, cs.shape[4])
-    n = 3 * LANES
-    near = jnp.dot(rows[:, :n], joined(pieces[:3]), preferred_element_type=F32)
-    m = rows.shape[1] - 2 * LANES
-    near += jnp.dot(rows[:, m:], joined(pieces[3:]), preferred_element_type=F32)
-    out[...] = near.reshape(out.shape)
-
-
-def late_kernel(dc, cs, early, *refs):
-    pieces, out = refs[:-1], refs[-1]
+    n, m = 3 * LANES, rows.shape[1] - 3 * LANES
+    parts = [rows[:, :n], rows[:, n + LANES : m], rows[:, m + LANES :]]
+    part = jnp.dot(jnp.concatenate(parts, 1), joined(pieces), preferred_element_type=F32)
+    out[...] = part.reshape(out.shape)
+
+
+def late_kernel(dc, cs, early, ahead, behind, out):
     rows = cs[dc].reshape(-1, cs.shape[4])
-    m = rows.shape[1] - 2 * LANES
-    part = jnp.dot(rows[:, 3 * LANES : m], joined(pieces), preferred_element_type=F32)
+    n, m = 3 * LANES, rows.shape[1] - 3 * LANES
+    rows = jnp.concatenate([rows[:, n : n + LANES], rows[:, m : m + LANES]], 1)
+    part = jnp.dot(rows, joined([ahead, behind]), preferred_element_type=F32)
     out[...] = (part.reshape(out.shape) + early[dc]).astype(out.dtype)
 
 
@@ -170,12 +169,12 @@
     gp_out[...] = gp
 
 
-def grads_far_kernel(spec_scale, scal, cs, kvrel, stacked, gf_in, gp_in, *refs):
+def grads_far_kernel(scal, cs, kvrel, stacked, gf_in, gp_in, *refs):
     pieces, out = refs[:-1], refs[-1]
     beads_all = joined(pieces)
     gf, gp = half_gradients(1, cs, kvrel, stacked, beads_all)
-    gf = ((gf + gf_in[...]) * spec_scale).astype(BF16)
-    gp = (gp + gp_in[...]) * spec_scale
+    gf = (gf + gf_in[...]).astype(BF16)
+    gp = gp + gp_in[...]
     hi = gp.astype(BF16).astype(F32)
     tail = jnp.concatenate([hi[0:3], (gp - hi)[0:3], jnp.zeros_like(gp[0:2])], 0).astype(BF16)
     n_z = out.shape[0]
@@ -188,13 +187,15 @@
         out[to, width : width + 8, :] = tail[:, at]
 
 
-def total_kernel(arrived, gf_out, gp_out):
+def total_kernel(spec_scale, arrived, grad_filter, gf_out, gp_out, filter_out):
     total = arrived[0].astype(F32)
     for i in range(1, arrived.shape[0]):
         total = total + arrived[i].astype(F32)
+    total = total * spec_scale
     width = gf_out.shape[1]
     gf_out[...] = total[:width].T.astype(BF16)
     gp_out[...] = total[width : width + 3] + total[width + 3 : width + 6]
+    filter_out[...] = grad_filter[...]
 
 
 def call(kernel, out_shape, n_in, scalars=0, scratch=(), aliases=None, space=pltpu.VMEM):
@@ -271,14 +272,14 @@
     pairs = [(at(z, c), at((z + 2 - 4 * c) % n_z, c)) for z in range(n_z) for c in range(2)]
     pieces[4] = lax.ppermute(onward, ("zh", "core", "zl"), pairs)
     pieces[3], pieces[5] = along_z(ahead, 1), along_z(behind, -1)
-    late_blocks = [pieces[3], pieces[4], pieces[5]]
+    late_blocks = [pieces[3], pieces[5]]
     blocks = [pieces[k] for k in range(n_z)]
     cs = call(trig_far_kernel, cs_shape, 5, scalars=1, aliases={4: 0})(
         scal, pieces[2], pieces[6], trig[2], trig[0]
     )
     kvrel = trig[1]
 
-    near_blocks = blocks[:3] + blocks[-2:]
+    near_blocks = [blocks[k] for k in range(n_z) if k not in (3, n_z - 3)]
     early = call(
         early_kernel, shape((2, n_xy, 32, 2 * width), F32), 1 + len(near_blocks)
     )(cs, *near_blocks)
@@ -306,15 +307,19 @@
         3 + len(blocks),
     )(cs, kvrel, near, *blocks)
     parts = call(
-        lambda *refs: grads_far_kernel(spec_scale, *refs),
+        grads_far_kernel,
         shape((n_z, width + 8, beads_dev), BF16),
         6 + len(blocks),
         scalars=1,
     )(scal, cs, kvrel, far, gf, gp, *blocks)
-    grad_feat, grad_pos = call(
-        total_kernel, (shape((beads_dev, width), BF16), shape((3, beads_dev), F32)), 1
-    )(lax.all_to_all(parts, Z, 0, 0, tiled=True))
-    return grad_feat, grad_pos, grad_filter
+    outs = (
+        shape((beads_dev, width), BF16),
+        shape((3, beads_dev), F32),
+        shape((16, width), F32),
+    )
+    return call(lambda *refs: total_kernel(spec_scale, *refs), outs, 2)(
+        lax.all_to_all(parts, Z, 0, 0, tiled=True), grad_filter
+    )
 
 
 def solution(mesh):

time: 91.6 us -> 90.1 us (0.984)
  blocking collectives: 53.7 us -> 52.3 us
  starting transfers between devices: 14.1 us -> 15.3 us
    ppermute x6, starting transfers between devices: 11.3 us -> 15.1 us  [along_z(): return lax.ppermute(a, Z, [(i, (i + k) % n_z) for i in range(n_z)])]
    ppermute x1, starting transfers between devices: 2.66 us -> 0.08 us  [body(): pieces[4] = lax.ppermute(onward, ('zh', 'core', 'zl'), pairs)]
    ppermute x1, waiting for transfers between devices: 1.73 us -> 0.16 us  [body(): pieces[4] = lax.ppermute(onward, ('zh', 'core', 'zl'), pairs)]
    all_to_all x1, blocking collectives: 22.2 us -> 20.8 us  [body(): lax.all_to_all(parts, Z, 0, 0, tiled=True)]
where the time goes in v1:
time: 90.1 us; the launch traced here: 88.6 us
  blocking collectives  52.3 us (58%)
  starting transfers between devices  15.3 us (17%)
  Pallas kernels  11.6 us (13%)
  waiting for transfers between devices  8.33 us (9%)
    all_to_all x1, blocking collectives, body(): lax.all_to_all(parts, Z, 0, 0, tiled=True)  20.8 us
    all_to_all x1, blocking collectives, body(): arrived = lax.all_to_all(mine, XY, 0, 0, tiled=True)  17.6 us
    ppermute x6, starting transfers between devices, along_z(): return lax.ppermute(a, Z, [(i, (i + k) % n_z) for i in range(n_z)])  15.1 us
    all_to_all x1, blocking collectives, body(): near = lax.all_to_all(copies, XY, 0, 0, tiled=True)  13.9 us
    ppermute x6, waiting for transfers between devices, along_z(): return lax.ppermute(a, Z, [(i, (i + k) % n_z) for i in range(n_z)])  5.86 us
    pallas_call x1, Pallas kernels, body(): call(trig_near_kernel, (cs_shape, shape((n_rows, 16), BF16), shape((n_row...  2.8 us
    pallas_call x1, Pallas kernels, body(): call(trig_far_kernel, cs_shape, 5, scalars=1, aliases={4: 0})  2.35 us
    ppermute x2, waiting for transfers between devices, across(): return lax.ppermute(a, 'core', [(0, 1), (1, 0)])  2.3 us
  transfers between devices with their start and end apart: 9, of which 5 were waited for; matrix products, arithmetic and copies ran while one was open for 0% of the time, Pallas kernels for 9%

profile of v1, /device:TPU:8, one launch (start us, length us, event | category | flops | bytes accessed | tf_op | source)
XLA Modules:
  0.0 88.6 jit_solution(12847381610038157736)
XLA Ops:
  0.6 1.0 %shard_map.76 = (bf16[128,512]{1,0:T(8,128)(2,1)S(1)}, bf16[144,512]{1,0:T(8,128)(2,1)S(1)}, f32[3,512]{1,0:T(4,128)S(1)}, f32[3,4096]{1,0:T(4,128)S(1)}) custom-call(bf16[128,256]{1,0:T(8,128)(2,1)} %cot.1, bf16[128,256]{1,0:T(8,128)(2,1)} %feat.1, f32[3,512]{1,0:T(4,128)} %pos.1, f32[3,4096]{1,0:T(4,128)} %wv.1), custom_call_target="tpu_custom_call" | custom-call | tf_op jit(solution)/shard_map/pallas_call | solution.py:237
  1.6 6.4 %collective-permute-start.1 = (bf16[144,512]{1,0:T(8,128)(2,1)S(1)}, bf16[144,512]{1,0:T(8,128)(2,1)S(1)}, u32[]{:S(2)}, u32[]{:S(2)}) collective-permute-start(bf16[144,512]{1,0:T(8,128)(2,1)S(1)} %get-tuple-element.23), channel_id=1, source_target_pairs={{0,10},{1,11},{2,0},{3,1},{8,2},{9,3},{10,8},{11,9},{4,14},{5,15},... | collective-permute-start | bytes 442376 | tf_op jit(solution)/shard_map/ppermute | solution.py:230
  8.0 0.0 collective-permute-start
  8.0 0.1 pad_add_fusion.scal
  8.1 2.8 %shard_map.77 = (bf16[2,16,2,16,1024]{4,3,2,1,0:T(8,128)(2,1)S(1)}, bf16[512,16]{1,0:T(8,128)(2,1)S(1)}, f32[512,8]{1,0:T(8,128)S(1)}) custom-call(s32[3]{0:T(128)S(1)} %pad_add_fusion.scal, f32[3,512]{1,0:T(4,128)S(1)} %get-tuple-element.25.pos, f32[3,4096]{1,0:T(4,128)S(1)} %get-tuple-element.26.wv), custom_call_target="tpu_custom_call" | custom-call | tf_op jit(solution)/shard_map/pallas_call | solution.py:255
  10.9 3.8 %collective-permute-start.4 = (bf16[128,512]{1,0:T(8,128)(2,1)S(1)}, bf16[128,512]{1,0:T(8,128)(2,1)S(1)}, u32[]{:S(2)}, u32[]{:S(2)}) collective-permute-start(bf16[128,512]{1,0:T(8,128)(2,1)S(1)} %get-tuple-element.38.refs_0_), channel_id=1, source_target_pairs={{0,11},{1,0},{2,1},{3,2},{8,3},{9,8},{10,9},{11,10},{4,15},{5,4},{... | collective-permute-start | bytes 393224 | tf_op jit(solution)/shard_map/ppermute | solution.py:230
  14.7 0.0 collective-permute-start.2
  14.7 0.0 collective-permute-done.1.behind.refs_4_.refs_6_
  14.7 3.2 %collective-permute-done.ahead.refs_2_ = bf16[144,512]{1,0:T(8,128)(2,1)S(1)} collective-permute-done((bf16[144,512]{1,0:T(8,128)(2,1)S(1)}, bf16[144,512]{1,0:T(8,128)(2,1)S(1)}, u32[]{:S(2)}, u32[]{:S(2)}) %collective-permute-start) | collective-permute-done | bytes 147488 | tf_op jit(solution)/shard_map/ppermute | solution.py:230
  17.9 0.1 collective-permute-start.3
  18.0 5.0 %collective-permute-start.6 = (bf16[128,512]{1,0:T(8,128)(2,1)S(1)}, bf16[128,512]{1,0:T(8,128)(2,1)S(1)}, u32[]{:S(2)}, u32[]{:S(2)}) collective-permute-start(bf16[128,512]{1,0:T(8,128)(2,1)S(1)} %get-tuple-element.43), channel_id=1, source_target_pairs={{0,11},{1,0},{2,1},{3,2},{8,3},{9,8},{10,9},{11,10},{4,15},{5,4},{... | collective-permute-start | bytes 393224 | tf_op jit(solution)/shard_map/ppermute | solution.py:230
  23.0 0.0 collective-permute-start.5
  23.0 2.4 %shard_map.78.cs.refs_0_ = bf16[2,16,2,16,1024]{4,3,2,1,0:T(8,128)(2,1)S(1)} custom-call(s32[3]{0:T(128)S(1)} %pad_add_fusion.scal, bf16[144,512]{1,0:T(8,128)(2,1)S(1)} %collective-permute-done.ahead.refs_2_, bf16[144,512]{1,0:T(8,128)(2,1)S(1)} %collective-permute-done.1.behind.refs_4_.refs_6_, ...), custom_call_target="tpu_custom_call", output_to_operand_aliasing={{}: (4, {})} | custom-call | tf_op jit(solution)/shard_map/pallas_call | solution.py:277
  25.3 0.0 collective-permute-done.4.refs_5_.refs_7_
  25.3 0.0 collective-permute-done.2.refs_1_
  25.3 0.2 collective-permute-done.3.refs_3_.refs_4_
  25.5 1.0 %shard_map.79.refs_1_ = f32[2,16,32,512]{3,2,1,0:T(8,128)S(1)} custom-call(bf16[2,16,2,16,1024]{4,3,2,1,0:T(8,128)(2,1)S(1)} %shard_map.78.cs.refs_0_, bf16[128,512]{1,0:T(8,128)(2,1)S(1)} %get-tuple-element.38.refs_0_, bf16[128,512]{1,0:T(8,128)(2,1)S(1)} %collective-permute-done.2.refs_1_, bf16[144,512]{1,0:T(8,128)(2,1)S(1)} %collective-permute-done.ahead.refs_2_, ...), custom_call_target="tpu_custom_call" | custom-call | tf_op jit(solution)/shard_map/pallas_call | solution.py:283
  26.5 0.0 collective-permute-done.6.refs_3_.refs_5_
  26.5 2.6 %collective-permute-done.5.refs_2_.refs_3_ = bf16[128,512]{1,0:T(8,128)(2,1)S(1)} collective-permute-done((bf16[128,512]{1,0:T(8,128)(2,1)S(1)}, bf16[128,512]{1,0:T(8,128)(2,1)S(1)}, u32[]{:S(2)}, u32[]{:S(2)}) %collective-permute-start.5) | collective-permute-done | bytes 131104 | tf_op jit(solution)/shard_map/ppermute | solution.py:230
  29.1 0.3 shard_map.81
  29.4 0.1 collective-permute-start.7
  29.5 0.3 shard_map.80
  29.8 0.0 copy-start
  29.8 1.6 %collective-permute-done.7 = bf16[16,32,512]{2,1,0:T(8,128)(2,1)S(1)} collective-permute-done((bf16[16,32,512]{2,1,0:T(8,128)(2,1)S(1)}, bf16[16,32,512]{2,1,0:T(8,128)(2,1)S(1)}, u32[]{:S(2)}, u32[]{:S(2)}) %collective-permute-start.7) | collective-permute-done | bytes 524320 | tf_op jit(solution)/shard_map/ppermute | solution.py:233
  31.4 0.2 add_convert_fusion
  31.6 17.6 %all_to_all.15.refs_0_ = bf16[16,32,512]{2,1,0:T(8,128)(2,1)S(1)} all-to-all(bf16[16,32,512]{2,1,0:T(8,128)(2,1)S(1)} %add_convert_fusion), channel_id=1, replica_groups=mesh['x'=4,'y'=4,'zh'=2,'core'=2,'zl'=4] {'x','y'}, dimensions={0} | all-to-all | bytes 1048576 | tf_op jit(solution)/shard_map/all_to_all | solution.py:296
  49.2 0.0 copy-done
  49.2 0.1 shard_map.82
  49.4 13.9 %all_to_all.16.stacked = bf16[16,32,512]{2,1,0:T(8,128)(2,1)S(1)} all-to-all(bf16[16,32,512]{2,1,0:T(8,128)(2,1)S(1)} %get-tuple-element.39), channel_id=1, replica_groups=mesh['x'=4,'y'=4,'zh'=2,'core'=2,'zl'=4] {'x','y'}, dimensions={0} | all-to-all | bytes 1048576 | tf_op jit(solution)/shard_map/all_to_all | solution.py:302
  63.3 0.0 collective-permute-start.8
  63.3 1.2 %shard_map.83 = (f32[256,1024]{1,0:T(8,128)S(1)}, f32[8,1024]{1,0:T(8,128)S(1)}) custom-call(bf16[2,16,2,16,1024]{4,3,2,1,0:T(8,128)(2,1)S(1)} %shard_map.78.cs.refs_0_, bf16[512,16]{1,0:T(8,128)(2,1)S(1)} %get-tuple-element.37.kvrel, bf16[16,32,512]{2,1,0:T(8,128)(2,1)S(1)} %all_to_all.16.stacked, bf16[128,512]{1,0:T(8,128)(2,1)S(1)} %get-tuple-element.38.refs_0_, ...), custom_call_target="tpu_custom_call" | custom-call | tf_op jit(solution)/shard_map/pallas_call | solution.py:304
  64.5 0.7 collective-permute-done.8.stacked
  65.2 1.8 %shard_map.84 = bf16[8,264,128]{2,1,0:T(8,128)(2,1)S(1)} custom-call(s32[3]{0:T(128)S(1)} %pad_add_fusion.scal, bf16[2,16,2,16,1024]{4,3,2,1,0:T(8,128)(2,1)S(1)} %shard_map.78.cs.refs_0_, bf16[512,16]{1,0:T(8,128)(2,1)S(1)} %get-tuple-element.37.kvrel, bf16[16,32,512]{2,1,0:T(8,128)(2,1)S(1)} %collective-permute-done.8.stacked, ...), custom_call_target="tpu_custom_call" | custom-call | tf_op jit(solution)/shard_map/pallas_call | solution.py:309
  67.0 20.8 %all_to_all.17.refs_0_ = bf16[8,264,128]{2,1,0:T(8,128)(2,1)S(1)} all-to-all(bf16[8,264,128]{2,1,0:T(8,128)(2,1)S(1)} %shard_map.84), channel_id=1, replica_groups=mesh['x'=4,'y'=4,'zh'=2,'core'=2,'zl'=4] {'zh','zl'}, dimensions={0} | all-to-all | bytes 1081344 | tf_op jit(solution)/shard_map/all_to_all | solution.py:321
  87.8 0.8 shard_map.85
  (1 shorter events, 0.0 us)
Async XLA Ops:
  1.6 13.0 %collective-permute-start.1 = (bf16[144,512]{1,0:T(8,128)(2,1)S(1)}, bf16[144,512]{1,0:T(8,128)(2,1)S(1)}, u32[]{:S(2)}, u32[]{:S(2)}) collective-permute-start(bf16[144,512]{1,0:T(8,128)(2,1)S(1)} %get-tuple-element.23), channel_id=1, source_target_pairs={{0,10},{1,11},{2,0},{3,1},{8,2},{9,3},{10,8},{11,9},{4,14},{5,15},... | collective-permute-start | bytes 442376 | tf_op jit(solution)/shard_map/ppermute | solution.py:230
  8.0 9.9 %collective-permute-start = (bf16[144,512]{1,0:T(8,128)(2,1)S(1)}, bf16[144,512]{1,0:T(8,128)(2,1)S(1)}, u32[]{:S(2)}, u32[]{:S(2)}) collective-permute-start(bf16[144,512]{1,0:T(8,128)(2,1)S(1)} %get-tuple-element.23), channel_id=1, source_target_pairs={{0,2},{1,3},{2,8},{3,9},{8,10},{9,11},{10,0},{11,1},{4,6},{5,7},{6... | collective-permute-start | bytes 442376 | tf_op jit(solution)/shard_map/ppermute | solution.py:230
  10.9 14.4 %collective-permute-start.4 = (bf16[128,512]{1,0:T(8,128)(2,1)S(1)}, bf16[128,512]{1,0:T(8,128)(2,1)S(1)}, u32[]{:S(2)}, u32[]{:S(2)}) collective-permute-start(bf16[128,512]{1,0:T(8,128)(2,1)S(1)} %get-tuple-element.38.refs_0_), channel_id=1, source_target_pairs={{0,11},{1,0},{2,1},{3,2},{8,3},{9,8},{10,9},{11,10},{4,15},{5,4},{... | collective-permute-start | bytes 393224 | tf_op jit(solution)/shard_map/ppermute | solution.py:230
  14.7 10.7 %collective-permute-start.2 = (bf16[128,512]{1,0:T(8,128)(2,1)S(1)}, bf16[128,512]{1,0:T(8,128)(2,1)S(1)}, u32[]{:S(2)}, u32[]{:S(2)}) collective-permute-start(bf16[128,512]{1,0:T(8,128)(2,1)S(1)} %get-tuple-element.38.refs_0_), channel_id=1, source_target_pairs={{0,1},{1,2},{2,3},{3,8},{8,9},{9,10},{10,11},{11,0},{4,5},{5,6},{6... | collective-permute-start | bytes 393224 | tf_op jit(solution)/shard_map/ppermute | solution.py:230
  17.9 7.6 %collective-permute-start.3 = (bf16[128,512]{1,0:T(8,128)(2,1)S(1)}, bf16[128,512]{1,0:T(8,128)(2,1)S(1)}, u32[]{:S(2)}, u32[]{:S(2)}) collective-permute-start(bf16[128,512]{1,0:T(8,128)(2,1)S(1)} %get-tuple-element.44), channel_id=1, source_target_pairs={{0,2},{4,14},{1,3},{5,15},{2,8},{6,4},{3,9},{7,5},{8,10},{12,6},{9... | collective-permute-start | bytes 393224 | tf_op jit(solution)/shard_map/ppermute | solution.py:273
  18.0 8.5 %collective-permute-start.6 = (bf16[128,512]{1,0:T(8,128)(2,1)S(1)}, bf16[128,512]{1,0:T(8,128)(2,1)S(1)}, u32[]{:S(2)}, u32[]{:S(2)}) collective-permute-start(bf16[128,512]{1,0:T(8,128)(2,1)S(1)} %get-tuple-element.43), channel_id=1, source_target_pairs={{0,11},{1,0},{2,1},{3,2},{8,3},{9,8},{10,9},{11,10},{4,15},{5,4},{... | collective-permute-start | bytes 393224 | tf_op jit(solution)/shard_map/ppermute | solution.py:230
  23.0 6.2 %collective-permute-start.5 = (bf16[128,512]{1,0:T(8,128)(2,1)S(1)}, bf16[128,512]{1,0:T(8,128)(2,1)S(1)}, u32[]{:S(2)}, u32[]{:S(2)}) collective-permute-start(bf16[128,512]{1,0:T(8,128)(2,1)S(1)} %get-tuple-element.45), channel_id=1, source_target_pairs={{0,1},{1,2},{2,3},{3,8},{8,9},{9,10},{10,11},{11,0},{4,5},{5,6},{6... | collective-permute-start | bytes 393224 | tf_op jit(solution)/shard_map/ppermute | solution.py:230
  29.4 2.0 %collective-permute-start.7 = (bf16[16,32,512]{2,1,0:T(8,128)(2,1)S(1)}, bf16[16,32,512]{2,1,0:T(8,128)(2,1)S(1)}, u32[]{:S(2)}, u32[]{:S(2)}) collective-permute-start(bf16[16,32,512]{2,1,0:T(8,128)(2,1)S(1)} %shard_map.81), channel_id=1, source_target_pairs={{0,4},{4,0},{1,5},{5,1},{2,6},{6,2},{3,7},{7,3},{8,12},{12,8},{9,1... | collective-permute-start | bytes 1572872 | tf_op jit(solution)/shard_map/ppermute | solution.py:233
  29.8 19.4 %copy-start = (bf16[16,256]{1,0:T(8,128)(2,1)S(1)}, bf16[16,256]{1,0:T(8,128)(2,1)}, u32[]{:S(2)}) copy-start(bf16[16,256]{1,0:T(8,128)(2,1)} %refs_1_.1) | copy-start | bytes 24580
  63.3 1.9 %collective-permute-start.8 = (bf16[16,32,512]{2,1,0:T(8,128)(2,1)S(1)}, bf16[16,32,512]{2,1,0:T(8,128)(2,1)S(1)}, u32[]{:S(2)}, u32[]{:S(2)}) collective-permute-start(bf16[16,32,512]{2,1,0:T(8,128)(2,1)S(1)} %all_to_all.16.stacked), channel_id=1, source_target_pairs={{0,4},{4,0},{1,5},{5,1},{2,6},{6,2},{3,7},{7,3},{8,12},{12,8},{9,1... | collective-permute-start | bytes 1572872 | tf_op jit(solution)/shard_map/ppermute | solution.py:233

commit v2 on v1

--- a/solution.py
+++ b/solution.py
@@ -75,8 +75,8 @@
     lax.fori_loop(0, 2 * n_xy, step, 0, unroll=4)
 
 
-def trig_near_kernel(scal, pos, wv, cs, kvrel, kcols, kvt):
-    zh, zl, core = scal[0], scal[1], scal[2]
+def trig_near_kernel(pos, wv, cs, kvrel, kcols, kvt):
+    zh, zl, core = (lax.axis_index(a) for a in ("zh", "zl", "core"))
     n_xy = cs.shape[1]
     n_zl = cs.shape[4] // LANES // 2
     for xy in range(n_xy):
@@ -96,8 +96,8 @@
     trig_rows(kcols, pos[...], cs, zh, zl, zh * n_zl)
 
 
-def trig_far_kernel(scal, ahead, behind, kcols, _, cs):
-    zh, zl = scal[0], scal[1]
+def trig_far_kernel(ahead, behind, kcols, _, cs):
+    zh, zl = lax.axis_index("zh"), lax.axis_index("zl")
     n_zl = cs.shape[4] // LANES // 2
     beads = ahead.shape[0] - 16
     rows = jnp.where(zl < n_zl // 2, ahead[beads:, :], behind[beads:, :]).astype(F32)
@@ -169,7 +169,7 @@
     gp_out[...] = gp
 
 
-def grads_far_kernel(scal, cs, kvrel, stacked, gf_in, gp_in, *refs):
+def grads_far_kernel(cs, kvrel, stacked, gf_in, gp_in, *refs):
     pieces, out = refs[:-1], refs[-1]
     beads_all = joined(pieces)
     gf, gp = half_gradients(1, cs, kvrel, stacked, beads_all)
@@ -179,7 +179,7 @@
     tail = jnp.concatenate([hi[0:3], (gp - hi)[0:3], jnp.zeros_like(gp[0:2])], 0).astype(BF16)
     n_z = out.shape[0]
     width = gf.shape[0]
-    here = scal[0] * (n_z // 2) + scal[1]
+    here = lax.axis_index(Z)
     for shift in range(n_z):
         at = slice(shift * LANES, (shift + 1) * LANES)
         to = lax.rem(here + n_z - shift, n_z)
@@ -198,9 +198,8 @@
     filter_out[...] = grad_filter[...]
 
 
-def call(kernel, out_shape, n_in, scalars=0, scratch=(), aliases=None, space=pltpu.VMEM):
-    specs = [pl.BlockSpec(memory_space=pltpu.SMEM)] * scalars
-    specs += [pl.BlockSpec(memory_space=space)] * (n_in - scalars)
+def call(kernel, out_shape, n_in, scratch=(), aliases=None, space=pltpu.VMEM):
+    specs = [pl.BlockSpec(memory_space=space)] * n_in
     outs = jax.tree.map(lambda _: pl.BlockSpec(memory_space=pltpu.VMEM), out_shape)
     return pl.pallas_call(
         kernel,
@@ -248,17 +247,14 @@
     )(*inputs)
     pieces = {0: own, 2: along_z(sent, 2), 6: along_z(sent, -2)}
 
-    scal = jnp.stack([lax.axis_index("zh"), lax.axis_index("zl"), lax.axis_index("core")])
-    scal = scal.astype(jnp.int32)
     n_rows = 2 * n_xy * 16
     cs_shape = shape((2, n_xy, 2, 16, beads_grp), BF16)
     trig = call(
         trig_near_kernel,
         (cs_shape, shape((n_rows, 16), BF16), shape((n_rows, 8), F32)),
-        3,
-        scalars=1,
+        2,
         scratch=[pltpu.VMEM((n_xy, LANES, 8), F32)],
-    )(scal, pos_near, wv_near)
+    )(pos_near, wv_near)
     own, trig = lax.optimization_barrier((own, trig))
     pieces[1], pieces[7] = along_z(own, 1), along_z(own, -1)
     pieces[2], pieces[6], trig = lax.optimization_barrier((pieces[2], pieces[6], trig))
@@ -274,8 +270,8 @@
     pieces[3], pieces[5] = along_z(ahead, 1), along_z(behind, -1)
     late_blocks = [pieces[3], pieces[5]]
     blocks = [pieces[k] for k in range(n_z)]
-    cs = call(trig_far_kernel, cs_shape, 5, scalars=1, aliases={4: 0})(
-        scal, pieces[2], pieces[6], trig[2], trig[0]
+    cs = call(trig_far_kernel, cs_shape, 4, aliases={3: 0})(
+        pieces[2], pieces[6], trig[2], trig[0]
     )
     kvrel = trig[1]
 
@@ -309,9 +305,8 @@
     parts = call(
         grads_far_kernel,
         shape((n_z, width + 8, beads_dev), BF16),
-        6 + len(blocks),
-        scalars=1,
-    )(scal, cs, kvrel, far, gf, gp, *blocks)
+        5 + len(blocks),
+    )(cs, kvrel, far, gf, gp, *blocks)
     outs = (
         shape((beads_dev, width), BF16),
         shape((3, beads_dev), F32),

time: 90.1 us -> 89.5 us (level)
  Pallas kernels: 11.6 us -> 9.89 us
  waiting for transfers between devices: 8.33 us -> 9.7 us
    pallas_call x2, Pallas kernels: 4.12 us -> 3.02 us  [the longest x1 1.81 us: body(): call(trig_far_kernel, cs_shape, 4, aliases={3: 0})]
    ppermute x6, waiting for transfers between devices: 5.86 us -> 6.77 us  [along_z(): return lax.ppermute(a, Z, [(i, (i + k) % n_z) for i in range(n_z)])]
  transfers between devices with their start and end apart: 9 -> 9, of which waited for: 5 -> 6; matrix products, arithmetic and copies ran while one was open for 0% -> 0% of each run, Pallas kernels for 9% -> 7%
where the time goes in v2:
time: 89.5 us; the launch traced here: 88.1 us
  blocking collectives  52.4 us (59%)
  starting transfers between devices  15.2 us (17%)
  Pallas kernels  9.89 us (11%)
  waiting for transfers between devices  9.7 us (11%)
    all_to_all x1, blocking collectives, body(): lax.all_to_all(parts, Z, 0, 0, tiled=True)  20.8 us
    all_to_all x1, blocking collectives, body(): arrived = lax.all_to_all(mine, XY, 0, 0, tiled=True)  17.6 us
    ppermute x6, starting transfers between devices, along_z(): return lax.ppermute(a, Z, [(i, (i + k) % n_z) for i in range(n_z)])  15 us
    all_to_all x1, blocking collectives, body(): near = lax.all_to_all(copies, XY, 0, 0, tiled=True)  13.9 us
    ppermute x6, waiting for transfers between devices, along_z(): return lax.ppermute(a, Z, [(i, (i + k) % n_z) for i in range(n_z)])  6.77 us
    ppermute x2, waiting for transfers between devices, across(): return lax.ppermute(a, 'core', [(0, 1), (1, 0)])  2.31 us
    pallas_call x1, Pallas kernels, body(): call(trig_near_kernel, (cs_shape, shape((n_rows, 16), BF16), shape((n_row...  2.26 us
    pallas_call x1, Pallas kernels, body(): call(trig_far_kernel, cs_shape, 4, aliases={3: 0})  1.81 us
  transfers between devices with their start and end apart: 9, of which 6 were waited for; matrix products, arithmetic and copies ran while one was open for 0% of the time, Pallas kernels for 7%

profile of v2, /device:TPU:8, one launch (start us, length us, event | category | flops | bytes accessed | tf_op | source)
XLA Modules:
  0.0 88.1 jit_solution(3156053415222817687)
XLA Ops:
  0.6 1.0 %shard_map.76 = (bf16[128,512]{1,0:T(8,128)(2,1)S(1)}, bf16[144,512]{1,0:T(8,128)(2,1)S(1)}, f32[3,512]{1,0:T(4,128)S(1)}, f32[3,4096]{1,0:T(4,128)S(1)}) custom-call(bf16[128,256]{1,0:T(8,128)(2,1)} %cot.1, bf16[128,256]{1,0:T(8,128)(2,1)} %feat.1, f32[3,512]{1,0:T(4,128)} %pos.1, f32[3,4096]{1,0:T(4,128)} %wv.1), custom_call_target="tpu_custom_call" | custom-call | tf_op jit(solution)/shard_map/pallas_call | solution.py:236
  1.6 6.4 %collective-permute-start.1 = (bf16[144,512]{1,0:T(8,128)(2,1)S(1)}, bf16[144,512]{1,0:T(8,128)(2,1)S(1)}, u32[]{:S(2)}, u32[]{:S(2)}) collective-permute-start(bf16[144,512]{1,0:T(8,128)(2,1)S(1)} %get-tuple-element.23), channel_id=1, source_target_pairs={{0,10},{1,11},{2,0},{3,1},{8,2},{9,3},{10,8},{11,9},{4,14},{5,15},... | collective-permute-start | bytes 442376 | tf_op jit(solution)/shard_map/ppermute | solution.py:229
  8.0 0.0 collective-permute-start
  8.0 2.3 %shard_map.77 = (bf16[2,16,2,16,1024]{4,3,2,1,0:T(8,128)(2,1)S(1)}, bf16[512,16]{1,0:T(8,128)(2,1)S(1)}, f32[512,8]{1,0:T(8,128)S(1)}) custom-call(f32[3,512]{1,0:T(4,128)S(1)} %get-tuple-element.25.pos, f32[3,4096]{1,0:T(4,128)S(1)} %get-tuple-element.26.wv), custom_call_target="tpu_custom_call" | custom-call | tf_op jit(solution)/shard_map/pallas_call | solution.py:252
  10.3 3.8 %collective-permute-start.4 = (bf16[128,512]{1,0:T(8,128)(2,1)S(1)}, bf16[128,512]{1,0:T(8,128)(2,1)S(1)}, u32[]{:S(2)}, u32[]{:S(2)}) collective-permute-start(bf16[128,512]{1,0:T(8,128)(2,1)S(1)} %get-tuple-element.38.refs_0_), channel_id=1, source_target_pairs={{0,11},{1,0},{2,1},{3,2},{8,3},{9,8},{10,9},{11,10},{4,15},{5,4},{... | collective-permute-start | bytes 393224 | tf_op jit(solution)/shard_map/ppermute | solution.py:229
  14.0 0.0 collective-permute-start.2
  14.0 0.8 collective-permute-done.1.behind.refs_4_.refs_6_
  14.8 3.2 %collective-permute-done.ahead.refs_2_ = bf16[144,512]{1,0:T(8,128)(2,1)S(1)} collective-permute-done((bf16[144,512]{1,0:T(8,128)(2,1)S(1)}, bf16[144,512]{1,0:T(8,128)(2,1)S(1)}, u32[]{:S(2)}, u32[]{:S(2)}) %collective-permute-start) | collective-permute-done | bytes 147488 | tf_op jit(solution)/shard_map/ppermute | solution.py:229
  18.1 0.1 collective-permute-start.3
  18.2 4.8 %collective-permute-start.6 = (bf16[128,512]{1,0:T(8,128)(2,1)S(1)}, bf16[128,512]{1,0:T(8,128)(2,1)S(1)}, u32[]{:S(2)}, u32[]{:S(2)}) collective-permute-start(bf16[128,512]{1,0:T(8,128)(2,1)S(1)} %get-tuple-element.43), channel_id=1, source_target_pairs={{0,11},{1,0},{2,1},{3,2},{8,3},{9,8},{10,9},{11,10},{4,15},{5,4},{... | collective-permute-start | bytes 393224 | tf_op jit(solution)/shard_map/ppermute | solution.py:229
  23.0 0.0 collective-permute-start.5
  23.0 1.8 %shard_map.78.cs.refs_0_ = bf16[2,16,2,16,1024]{4,3,2,1,0:T(8,128)(2,1)S(1)} custom-call(bf16[144,512]{1,0:T(8,128)(2,1)S(1)} %collective-permute-done.ahead.refs_2_, bf16[144,512]{1,0:T(8,128)(2,1)S(1)} %collective-permute-done.1.behind.refs_4_.refs_6_, f32[512,8]{1,0:T(8,128)S(1)} %get-tuple-element.35.kcols, ...), custom_call_target="tpu_custom_call", output_to_operand_aliasing={{}: (3, {})} | custom-call | tf_op jit(solution)/shard_map/pallas_call | solution.py:273
  24.9 0.0 collective-permute-done.4.refs_5_.refs_7_
  24.9 0.0 collective-permute-done.2.refs_1_
  24.9 0.6 collective-permute-done.3.refs_3_.refs_4_
  25.5 1.0 %shard_map.79.refs_1_ = f32[2,16,32,512]{3,2,1,0:T(8,128)S(1)} custom-call(bf16[2,16,2,16,1024]{4,3,2,1,0:T(8,128)(2,1)S(1)} %shard_map.78.cs.refs_0_, bf16[128,512]{1,0:T(8,128)(2,1)S(1)} %get-tuple-element.38.refs_0_, bf16[128,512]{1,0:T(8,128)(2,1)S(1)} %collective-permute-done.2.refs_1_, bf16[144,512]{1,0:T(8,128)(2,1)S(1)} %collective-permute-done.ahead.refs_2_, ...), custom_call_target="tpu_custom_call" | custom-call | tf_op jit(solution)/shard_map/pallas_call | solution.py:279
  26.5 0.0 collective-permute-done.6.refs_3_.refs_5_
  26.5 2.7 %collective-permute-done.5.refs_2_.refs_3_ = bf16[128,512]{1,0:T(8,128)(2,1)S(1)} collective-permute-done((bf16[128,512]{1,0:T(8,128)(2,1)S(1)}, bf16[128,512]{1,0:T(8,128)(2,1)S(1)}, u32[]{:S(2)}, u32[]{:S(2)}) %collective-permute-start.5) | collective-permute-done | bytes 131104 | tf_op jit(solution)/shard_map/ppermute | solution.py:229
  29.2 0.3 shard_map.81
  29.5 0.1 collective-permute-start.7
  29.6 0.3 shard_map.80
  29.9 0.0 copy-start
  29.9 1.6 %collective-permute-done.7 = bf16[16,32,512]{2,1,0:T(8,128)(2,1)S(1)} collective-permute-done((bf16[16,32,512]{2,1,0:T(8,128)(2,1)S(1)}, bf16[16,32,512]{2,1,0:T(8,128)(2,1)S(1)}, u32[]{:S(2)}, u32[]{:S(2)}) %collective-permute-start.7) | collective-permute-done | bytes 524320 | tf_op jit(solution)/shard_map/ppermute | solution.py:232
  31.5 0.2 add_convert_fusion
  31.7 17.6 %all_to_all.15.refs_0_ = bf16[16,32,512]{2,1,0:T(8,128)(2,1)S(1)} all-to-all(bf16[16,32,512]{2,1,0:T(8,128)(2,1)S(1)} %add_convert_fusion), channel_id=1, replica_groups=mesh['x'=4,'y'=4,'zh'=2,'core'=2,'zl'=4] {'x','y'}, dimensions={0} | all-to-all | bytes 1048576 | tf_op jit(solution)/shard_map/all_to_all | solution.py:292
  49.3 0.0 copy-done
  49.3 0.1 shard_map.82
  49.4 13.9 %all_to_all.16.stacked = bf16[16,32,512]{2,1,0:T(8,128)(2,1)S(1)} all-to-all(bf16[16,32,512]{2,1,0:T(8,128)(2,1)S(1)} %get-tuple-element.39), channel_id=1, replica_groups=mesh['x'=4,'y'=4,'zh'=2,'core'=2,'zl'=4] {'x','y'}, dimensions={0} | all-to-all | bytes 1048576 | tf_op jit(solution)/shard_map/all_to_all | solution.py:298
  63.3 0.0 collective-permute-start.8
  63.3 1.2 %shard_map.83 = (f32[256,1024]{1,0:T(8,128)S(1)}, f32[8,1024]{1,0:T(8,128)S(1)}) custom-call(bf16[2,16,2,16,1024]{4,3,2,1,0:T(8,128)(2,1)S(1)} %shard_map.78.cs.refs_0_, bf16[512,16]{1,0:T(8,128)(2,1)S(1)} %get-tuple-element.37.kvrel, bf16[16,32,512]{2,1,0:T(8,128)(2,1)S(1)} %all_to_all.16.stacked, bf16[128,512]{1,0:T(8,128)(2,1)S(1)} %get-tuple-element.38.refs_0_, ...), custom_call_target="tpu_custom_call" | custom-call | tf_op jit(solution)/shard_map/pallas_call | solution.py:300
  64.5 0.7 collective-permute-done.8.stacked
  65.2 1.2 %shard_map.84 = bf16[8,264,128]{2,1,0:T(8,128)(2,1)S(1)} custom-call(bf16[2,16,2,16,1024]{4,3,2,1,0:T(8,128)(2,1)S(1)} %shard_map.78.cs.refs_0_, bf16[512,16]{1,0:T(8,128)(2,1)S(1)} %get-tuple-element.37.kvrel, bf16[16,32,512]{2,1,0:T(8,128)(2,1)S(1)} %collective-permute-done.8.stacked, f32[256,1024]{1,0:T(8,128)S(1)} %get-tuple-element.40.gf_in, ...), custom_call_target="tpu_custom_call" | custom-call | tf_op jit(solution)/shard_map/pallas_call | solution.py:305
  66.5 20.8 %all_to_all.17.refs_0_ = bf16[8,264,128]{2,1,0:T(8,128)(2,1)S(1)} all-to-all(bf16[8,264,128]{2,1,0:T(8,128)(2,1)S(1)} %shard_map.84), channel_id=1, replica_groups=mesh['x'=4,'y'=4,'zh'=2,'core'=2,'zl'=4] {'zh','zl'}, dimensions={0} | all-to-all | bytes 1081344 | tf_op jit(solution)/shard_map/all_to_all | solution.py:316
  87.3 0.8 shard_map.85
  (1 shorter events, 0.0 us)
Async XLA Ops:
  1.6 13.2 %collective-permute-start.1 = (bf16[144,512]{1,0:T(8,128)(2,1)S(1)}, bf16[144,512]{1,0:T(8,128)(2,1)S(1)}, u32[]{:S(2)}, u32[]{:S(2)}) collective-permute-start(bf16[144,512]{1,0:T(8,128)(2,1)S(1)} %get-tuple-element.23), channel_id=1, source_target_pairs={{0,10},{1,11},{2,0},{3,1},{8,2},{9,3},{10,8},{11,9},{4,14},{5,15},... | collective-permute-start | bytes 442376 | tf_op jit(solution)/shard_map/ppermute | solution.py:229
  8.0 10.1 %collective-permute-start = (bf16[144,512]{1,0:T(8,128)(2,1)S(1)}, bf16[144,512]{1,0:T(8,128)(2,1)S(1)}, u32[]{:S(2)}, u32[]{:S(2)}) collective-permute-start(bf16[144,512]{1,0:T(8,128)(2,1)S(1)} %get-tuple-element.23), channel_id=1, source_target_pairs={{0,2},{1,3},{2,8},{3,9},{8,10},{9,11},{10,0},{11,1},{4,6},{5,7},{6... | collective-permute-start | bytes 442376 | tf_op jit(solution)/shard_map/ppermute | solution.py:229
  10.3 14.6 %collective-permute-start.4 = (bf16[128,512]{1,0:T(8,128)(2,1)S(1)}, bf16[128,512]{1,0:T(8,128)(2,1)S(1)}, u32[]{:S(2)}, u32[]{:S(2)}) collective-permute-start(bf16[128,512]{1,0:T(8,128)(2,1)S(1)} %get-tuple-element.38.refs_0_), channel_id=1, source_target_pairs={{0,11},{1,0},{2,1},{3,2},{8,3},{9,8},{10,9},{11,10},{4,15},{5,4},{... | collective-permute-start | bytes 393224 | tf_op jit(solution)/shard_map/ppermute | solution.py:229
  14.0 10.8 %collective-permute-start.2 = (bf16[128,512]{1,0:T(8,128)(2,1)S(1)}, bf16[128,512]{1,0:T(8,128)(2,1)S(1)}, u32[]{:S(2)}, u32[]{:S(2)}) collective-permute-start(bf16[128,512]{1,0:T(8,128)(2,1)S(1)} %get-tuple-element.38.refs_0_), channel_id=1, source_target_pairs={{0,1},{1,2},{2,3},{3,8},{8,9},{9,10},{10,11},{11,0},{4,5},{5,6},{6... | collective-permute-start | bytes 393224 | tf_op jit(solution)/shard_map/ppermute | solution.py:229
  18.1 7.4 %collective-permute-start.3 = (bf16[128,512]{1,0:T(8,128)(2,1)S(1)}, bf16[128,512]{1,0:T(8,128)(2,1)S(1)}, u32[]{:S(2)}, u32[]{:S(2)}) collective-permute-start(bf16[128,512]{1,0:T(8,128)(2,1)S(1)} %get-tuple-element.44), channel_id=1, source_target_pairs={{0,2},{4,14},{1,3},{5,15},{2,8},{6,4},{3,9},{7,5},{8,10},{12,6},{9... | collective-permute-start | bytes 393224 | tf_op jit(solution)/shard_map/ppermute | solution.py:269
  18.2 8.3 %collective-permute-start.6 = (bf16[128,512]{1,0:T(8,128)(2,1)S(1)}, bf16[128,512]{1,0:T(8,128)(2,1)S(1)}, u32[]{:S(2)}, u32[]{:S(2)}) collective-permute-start(bf16[128,512]{1,0:T(8,128)(2,1)S(1)} %get-tuple-element.43), channel_id=1, source_target_pairs={{0,11},{1,0},{2,1},{3,2},{8,3},{9,8},{10,9},{11,10},{4,15},{5,4},{... | collective-permute-start | bytes 393224 | tf_op jit(solution)/shard_map/ppermute | solution.py:229
  23.0 6.2 %collective-permute-start.5 = (bf16[128,512]{1,0:T(8,128)(2,1)S(1)}, bf16[128,512]{1,0:T(8,128)(2,1)S(1)}, u32[]{:S(2)}, u32[]{:S(2)}) collective-permute-start(bf16[128,512]{1,0:T(8,128)(2,1)S(1)} %get-tuple-element.45), channel_id=1, source_target_pairs={{0,1},{1,2},{2,3},{3,8},{8,9},{9,10},{10,11},{11,0},{4,5},{5,6},{6... | collective-permute-start | bytes 393224 | tf_op jit(solution)/shard_map/ppermute | solution.py:229
  29.5 2.0 %collective-permute-start.7 = (bf16[16,32,512]{2,1,0:T(8,128)(2,1)S(1)}, bf16[16,32,512]{2,1,0:T(8,128)(2,1)S(1)}, u32[]{:S(2)}, u32[]{:S(2)}) collective-permute-start(bf16[16,32,512]{2,1,0:T(8,128)(2,1)S(1)} %shard_map.81), channel_id=1, source_target_pairs={{0,4},{4,0},{1,5},{5,1},{2,6},{6,2},{3,7},{7,3},{8,12},{12,8},{9,1... | collective-permute-start | bytes 1572872 | tf_op jit(solution)/shard_map/ppermute | solution.py:232
  29.9 19.4 %copy-start = (bf16[16,256]{1,0:T(8,128)(2,1)S(1)}, bf16[16,256]{1,0:T(8,128)(2,1)}, u32[]{:S(2)}) copy-start(bf16[16,256]{1,0:T(8,128)(2,1)} %refs_1_.1) | copy-start | bytes 24580
  63.3 1.9 %collective-permute-start.8 = (bf16[16,32,512]{2,1,0:T(8,128)(2,1)S(1)}, bf16[16,32,512]{2,1,0:T(8,128)(2,1)S(1)}, u32[]{:S(2)}, u32[]{:S(2)}) collective-permute-start(bf16[16,32,512]{2,1,0:T(8,128)(2,1)S(1)} %all_to_all.16.stacked), channel_id=1, source_target_pairs={{0,4},{4,0},{1,5},{5,1},{2,6},{6,2},{3,7},{7,3},{8,12},{12,8},{9,1... | collective-permute-start | bytes 1572872 | tf_op jit(solution)/shard_map/ppermute | solution.py:232
